TPU v7x, 32 devices: a whole 2x2x4 slice. The times are simulated.
32 devices in a mesh: group: 2 (over y), expert: 16 (over z, x, core).
Axes of the slice: x: 2, y: 2, z: 4, core: 2. Of those that a mesh axis runs over, the one named last changes fastest.
Arguments:
- tokens: bfloat16 [256, 7168], P(('group', 'expert')), parts along dimension 0, may hold values from -6 to 6
- expert_ids: int32 [256, 8], P(('group', 'expert')), parts along dimension 0, may hold values from 0 to 15, all different within a row; in each aligned block of 8 rows (0 to 7, 8 to 15, ...) at most 5 rows name the same one
- gate_probs: float32 [256, 8], P(('group', 'expert')), parts along dimension 0, may hold values from 0.05 to 0.6
- gate_proj: bfloat16 [7168, 32768], P(None, 'expert'), may hold values from -0.0625 to 0.0625
- up_proj: bfloat16 [7168, 32768], P(None, 'expert'), may hold values from -0.0625 to 0.0625
- down_proj: bfloat16 [32768, 7168], P('expert'), may hold values from -0.125 to 0.125
Outputs:
- mixed: bfloat16 [256, 7168], P(('group', 'expert')), parts along dimension 0
There are 2 independent parts, one for each index of `group`. A program takes and returns all parts, laid end to end along the dimension named above; an argument that names none is the same for every part. Nothing has to cross between parts.
Inputs may be any that keep to these rules, and one draw needn't show every extreme that they name: `expert_ids`: each row names 8 different experts. Among the 8 tokens of one device (aligned blocks of 8 rows) no expert is named by more than 5 tokens, a bound that some blocks reach.
All inputs are finite; a program needn't handle non-finite values.
Results may differ from a plain program's by a relative error of at most 0.0051.
Values may be sent and summed in bfloat16 or wider, within the bound.
No kernel may reach another device: no remote copies, remote signals or barrier semaphores. Data moves between devices by JAX's collectives and lax.ppermute only.
A program may use at most 192 MiB of HBM per device.

v0:
```python
import jax
import jax.numpy as jnp
from jax import lax
from jax.sharding import PartitionSpec as P

FF = 2048
EXPERTS = 16
CAP = 5


def shards(tokens, expert_ids, gate_probs, gate_proj, up_proj, down_proj):
    hid_count = gate_proj.shape[1]
    splits = FF // hid_count
    tok_count, model_width = tokens.shape
    devices = lax.axis_size("expert")
    picks = expert_ids[:, :, None] == jnp.arange(EXPERTS, dtype=jnp.int32)[None, None, :]
    chosen = jnp.sum(picks.astype(jnp.int32), axis=1)
    weight_te = jnp.sum(jnp.where(picks, gate_probs[:, :, None], 0.0), axis=1)
    slot_of = jnp.cumsum(chosen, axis=0) - 1
    placed = (chosen[:, :, None] == 1) & (
        slot_of[:, :, None] == jnp.arange(CAP, dtype=jnp.int32)[None, None, :]
    )
    picked = placed.astype(jnp.bfloat16)
    combine_w = jnp.where(placed, weight_te[:, :, None], 0.0)
    packed = jnp.einsum("tec,td->ecd", picked, tokens, preferred_element_type=jnp.float32).astype(
        jnp.bfloat16
    )
    outgoing = jnp.broadcast_to(packed[:, None], (EXPERTS, splits, CAP, model_width)).reshape(
        devices, CAP, model_width
    )
    blocks = lax.all_to_all(outgoing, "expert", split_axis=0, concat_axis=0, tiled=True)
    flat_rows = blocks.reshape(-1, model_width)
    gate_val = jnp.dot(flat_rows, gate_proj, preferred_element_type=jnp.float32)
    up_val = jnp.dot(flat_rows, up_proj, preferred_element_type=jnp.float32)
    hidden = (jax.nn.silu(gate_val) * up_val).astype(jnp.bfloat16)
    result = jnp.dot(hidden, down_proj, preferred_element_type=jnp.float32)
    partial_value = result.reshape(blocks.shape[0], blocks.shape[1], model_width)
    returned = lax.all_to_all(partial_value, "expert", split_axis=0, concat_axis=0, tiled=True)
    returned = returned.reshape(EXPERTS, splits, CAP, model_width)
    combined = jnp.einsum("tec,escd->td", combine_w, returned, precision=lax.Precision.HIGHEST)
    return combined.astype(jnp.bfloat16)


def solution(mesh):
    placed = (
        P(("group", "expert"), None),
        P(("group", "expert"), None),
        P(("group", "expert"), None),
        P(None, "expert"),
        P(None, "expert"),
        P("expert", None),
    )
    return jax.shard_map(
        shards, mesh=mesh, in_specs=placed, out_specs=P(("group", "expert"), None), check_vma=False
    )
```

profile of v0, /device:TPU:15, one launch (start us, length us, event | category | flops | bytes accessed | tf_op | source)
XLA Modules:
  0.0 180.2 jit_solution(9811228272586178524)
XLA Ops:
  0.0 0.0 copy-start
  0.0 0.8 convert_reduce_fusion
  0.8 0.0 copy-start.5
  0.9 0.0 copy-start.2
  0.9 0.6 copy-done.2
  1.5 0.0 copy-done
  1.5 0.5 convolution_convert_fusion
  2.0 0.7 copy.12
  2.6 0.0 copy-done.5
  2.6 48.0 %all_to_all.10 = bf16[16,5,7168]{2,1,0:T(8,128)(2,1)S(1)} all-to-all(bf16[16,5,7168]{2,1,0:T(8,128)(2,1)S(1)} %copy.12), channel_id=1, replica_groups=mesh['group'=2,'expert'=16] {'expert'}, dimensions={0} | all-to-all | bytes 2293760 | tf_op jit(solution)/shard_map/all_to_all | solution.py:31
  50.7 0.6 reshape.23
  51.2 12.9 %fusion.23 = f32[80,2048]{1,0:T(8,128)} fusion(bf16[80,7168]{1,0:T(8,128)(2,1)S(1)} %reshape.23, bf16[7168,2048]{1,0:T(8,128)(2,1)} %param.9), kind=kOutput, calls=%fused_computation.30 | convolution fusion | flops 2348810240 | bytes 31162368 | tf_op jit(solution)/shard_map/dot_general | solution.py:33
  64.1 21.0 %fusion.2 = f32[80,7168]{1,0:T(8,128)S(1)} fusion(bf16[2048,7168]{1,0:T(8,128)(2,1)} %param.11, bf16[80,7168]{1,0:T(8,128)(2,1)S(1)} %reshape.23, bf16[7168,2048]{1,0:T(8,128)(2,1)} %param.10, f32[80,2048]{1,0:T(8,128)} %fusion.23), kind=kOutput, calls=%fused_computation.5 | convolution fusion | flops 4698603520 | bytes 62816256 | tf_op jit(solution)/shard_map/dot_general | solution.py:36
  85.1 0.0 copy-start.1
  85.1 2.0 %reshape.24 = f32[16,5,7168]{2,1,0:T(8,128)} reshape(f32[80,7168]{1,0:T(8,128)S(1)} %fusion.2) | data formatting | bytes 4587520 | tf_op jit(solution)/shard_map/reshape | solution.py:37
  87.2 0.0 copy-start.4
  87.2 0.0 copy-start.7
  87.2 0.0 copy-start.3
  87.2 0.0 copy-start.6
  87.2 5.6 %all-to-all-start.1 = ((f32[16,5,7168]{2,1,0:T(8,128)}), f32[16,5,7168]{2,1,0:T(8,128)}, u32[]{:S(2)}, u32[]{:S(2)}) async-start(f32[16,5,7168]{2,1,0:T(8,128)} %reshape.24), calls=%async_computation.1 | async-start | bytes 7340032 | tf_op jit(solution)/shard_map/all_to_all | solution.py:38
  92.8 0.0 copy-done.4
  92.8 0.0 copy-done.7
  92.8 0.1 select_reduce_fusion
  92.9 81.1 %all-to-all-done.1 = f32[16,5,7168]{2,1,0:T(8,128)} async-done(((f32[16,5,7168]{2,1,0:T(8,128)}), f32[16,5,7168]{2,1,0:T(8,128)}, u32[]{:S(2)}, u32[]{:S(2)}) %all-to-all-start.1) | async-done | bytes 2293792 | tf_op jit(solution)/shard_map/all_to_all | solution.py:38
  174.0 0.0 copy-done.3
  174.0 0.0 copy-done.6
  174.0 6.2 %fusion = bf16[8,7168]{1,0:T(8,128)(2,1)} fusion(f32[16,5,7168]{2,1,0:T(8,128)} %all-to-all-done.1, f32[8,16]{1,0:T(8,128)S(1)} %select_reduce_fusion, s32[8,16]{1,0:T(8,128)S(1)} %copy-done.3, pred[8,16]{1,0:T(8,128)(4,1)S(1)} %copy-done.6), kind=kOutput, calls=%fused_computation.2 | convolution fusion | flops 55109504 | bytes 2409600 | tf_op jit(solution)/shard_map/tec,escd->td/dot_general | solution.py:40
  180.2 0.0 copy-done.1
  (3 shorter events, 0.0 us)
Async XLA Ops:
  0.0 1.5 copy-start
  0.8 1.8 copy-start.5
  0.9 0.6 copy-start.2
  85.1 95.1 %copy-start.1 = (bf16[8,7168]{1,0:T(8,128)(2,1)S(1)}, bf16[8,7168]{1,0:T(8,128)(2,1)}, u32[]{:S(2)}) copy-start(bf16[8,7168]{1,0:T(8,128)(2,1)} %param.6) | copy-start | bytes 344068
  87.2 5.6 %copy-start.4 = (s32[8,8]{1,0:T(8,128)S(1)}, s32[8,8]{1,0:T(8,128)}, u32[]{:S(2)}) copy-start(s32[8,8]{1,0:T(8,128)} %param.7) | copy-start | bytes 772
  87.2 5.6 %copy-start.7 = (f32[8,8]{1,0:T(8,128)S(1)}, f32[8,8]{1,0:T(8,128)}, u32[]{:S(2)}) copy-start(f32[8,8]{1,0:T(8,128)} %param.8) | copy-start | bytes 772
  87.2 86.8 %copy-start.3 = (s32[8,16]{1,0:T(8,128)S(1)}, s32[8,16]{1,0:T(8,128)}, u32[]{:S(2)}) copy-start(s32[8,16]{1,0:T(8,128)} %copy-done.2) | copy-start | bytes 1540
  87.2 86.8 %copy-start.6 = (pred[8,16]{1,0:T(8,128)(4,1)S(1)}, pred[8,16]{1,0:T(8,128)(4,1)}, u32[]{:S(2)}) copy-start(pred[8,16]{1,0:T(8,128)(4,1)} %copy-done.5) | copy-start | bytes 388
  87.2 86.8 %all-to-all-start.1 = ((f32[16,5,7168]{2,1,0:T(8,128)}), f32[16,5,7168]{2,1,0:T(8,128)}, u32[]{:S(2)}, u32[]{:S(2)}) async-start(f32[16,5,7168]{2,1,0:T(8,128)} %reshape.24), calls=%async_computation.1 | async-start | bytes 7340032 | tf_op jit(solution)/shard_map/all_to_all | solution.py:38
where the time goes:
time: 180 us
  waiting for transfers between devices  81.1 us (45%)
  blocking collectives  48 us (27%)
  matrix products  40.5 us (22%)
  starting transfers between devices  5.58 us (3%)
  local copies, waits for them, and re-layouts  3.86 us (2%)
    all_to_all x1, waiting for transfers between devices, shards(): lax.all_to_all(partial_value, 'expert', split_axis=0, concat_axis=0, tile...  81.1 us
    all_to_all x1, blocking collectives, shards(): lax.all_to_all(outgoing, 'expert', split_axis=0, concat_axis=0, tiled=True)  48 us
    dot_general x1, matrix products, shards(): result = jnp.dot(hidden, down_proj, preferred_element_type=jnp.float32)  21 us
    dot_general x1, matrix products, shards(): gate_val = jnp.dot(flat_rows, gate_proj, preferred_element_type=jnp.float32)  12.9 us
    dot_general x1, matrix products, shards(): jnp.einsum('tec,escd->td', combine_w, returned, precision=lax.Precision.H...  6.16 us
    all_to_all x1, starting transfers between devices, shards(): lax.all_to_all(partial_value, 'expert', split_axis=0, concat_axis=0, tile...  5.58 us
  transfers between devices with their start and end apart: 1, of which 1 were waited for; matrix products, arithmetic and copies ran while one was open for 0% of the time, Pallas kernels for 0%

commit v1 on v0

--- a/solution.py
+++ b/solution.py
@@ -28,7 +28,19 @@
     outgoing = jnp.broadcast_to(packed[:, None], (EXPERTS, splits, CAP, model_width)).reshape(
         devices, CAP, model_width
     )
-    blocks = lax.all_to_all(outgoing, "expert", split_axis=0, concat_axis=0, tiled=True)
+    ways, here = (lax.axis_size("expert"), lax.axis_index("expert"))
+    width = outgoing.shape[0] // ways
+    shape = list(outgoing.shape)
+    shape[0] = width
+    height = shape[0]
+    shape[0] = height * ways
+    full = jnp.zeros(shape, outgoing.dtype)
+    for mask in range(ways):
+        part = lax.dynamic_slice_in_dim(outgoing, (here ^ mask) * width, width, axis=0)
+        if mask:
+            part = lax.ppermute(part, "expert", [(d, d ^ mask) for d in range(ways)])
+        full = lax.dynamic_update_slice_in_dim(full, part, (here ^ mask) * height, axis=0)
+    blocks = full
     flat_rows = blocks.reshape(-1, model_width)
     gate_val = jnp.dot(flat_rows, gate_proj, preferred_element_type=jnp.float32)
     up_val = jnp.dot(flat_rows, up_proj, preferred_element_type=jnp.float32)

time: 180 us -> 196 us (1.089)
  blocking collectives: 48 us -> 0 us
  waiting for transfers between devices: 81.1 us -> 124 us
  starting transfers between devices: 5.58 us -> 24 us
  local copies, waits for them, and re-layouts: 3.86 us -> 6.16 us
    all_to_all x1 -> x0, blocking collectives: 48 us -> none  [shards(): lax.all_to_all(outgoing, 'expert', split_axis=0, concat_axis=0, tiled=True)]
    ppermute x0 -> x15, waiting for transfers between devices: none -> 42.7 us  [shards(): part = lax.ppermute(part, 'expert', [(d, d ^ mask) for d in range(ways)])]
    ppermute x0 -> x15, starting transfers between devices: none -> 17.7 us  [shards(): part = lax.ppermute(part, 'expert', [(d, d ^ mask) for d in range(ways)])]
    dynamic_slice x0 -> x1, local copies, waits for them, and re-layouts: none -> 2.7 us  [shards(): lax.dynamic_slice_in_dim(outgoing, (here ^ mask) * width, width, axis=0)]
  transfers between devices with their start and end apart: 1 -> 16, of which waited for: 1 -> 11; matrix products, arithmetic and copies ran while one was open for 0% -> 0% of each run, Pallas kernels for 0% -> 0%
where the time goes in v1:
time: 196 us
  waiting for transfers between devices  124 us (63%)
  matrix products  40.5 us (21%)
  starting transfers between devices  24 us (12%)
  local copies, waits for them, and re-layouts  6.16 us (3%)
    all_to_all x1, waiting for transfers between devices, shards(): lax.all_to_all(partial_value, 'expert', split_axis=0, concat_axis=0, tile...  81.3 us
    ppermute x15, waiting for transfers between devices, shards(): part = lax.ppermute(part, 'expert', [(d, d ^ mask) for d in range(ways)])  42.7 us
    dot_general x1, matrix products, shards(): result = jnp.dot(hidden, down_proj, preferred_element_type=jnp.float32)  21 us
    ppermute x15, starting transfers between devices, shards(): part = lax.ppermute(part, 'expert', [(d, d ^ mask) for d in range(ways)])  17.7 us
    dot_general x1, matrix products, shards(): gate_val = jnp.dot(flat_rows, gate_proj, preferred_element_type=jnp.float32)  12.9 us
    all_to_all x1, starting transfers between devices, shards(): lax.all_to_all(partial_value, 'expert', split_axis=0, concat_axis=0, tile...  6.31 us
    dot_general x1, matrix products, shards(): jnp.einsum('tec,escd->td', combine_w, returned, precision=lax.Precision.H...  6.16 us
  transfers between devices with their start and end apart: 16, of which 11 were waited for; matrix products, arithmetic and copies ran while one was open for 0% of the time, Pallas kernels for 0%

profile of v1, /device:TPU:15, one launch (start us, length us, event | category | flops | bytes accessed | tf_op | source)
XLA Modules:
  0.0 196.0 jit_solution(5580824444786270734)
XLA Ops:
  0.0 0.8 convert_reduce_fusion
  1.0 0.5 convolution_convert_fusion
  1.5 2.7 %constant_dynamic-slice_fusion = (bf16[1,5,7168]{2,0,1:T(2,128)(2,1)S(1)}, bf16[1,5,7168]{2,0,1:T(2,128)(2,1)S(1)}, bf16[1,5,7168]{2,0,1:T(2,128)(2,1)S(1)}, bf1...) fusion(bf16[16,5,7168]{2,0,1:T(8,128)(2,1)S(1)} %convolution_co, ...), kind=kLoop, calls=%fused_computation.36 | loop fusion | bytes 2293824 | tf_op jit(solution)/shard_map/dynamic_slice | solution.py:39
  4.2 0.7 collective-permute-start
  4.9 0.3 collective-permute-start.1
  5.2 1.4 collective-permute-start.2
  6.8 1.6 collective-permute-start.4
  8.7 0.2 collective-permute-start.5
  8.9 1.3 collective-permute-done.1
  10.3 1.3 collective-permute-start.6
  11.7 2.2 %collective-permute-done.2 = bf16[1,5,7168]{2,0,1:T(2,128)(2,1)S(1)} collective-permute-done((bf16[1,5,7168]{2,0,1:T(2,128)(2,1)S(1)}, bf16[1,5,7168]{2,0,1:T(2,128)(2,1)S(1)}, u32[]{:S(2)}, u32[]{:S(2)}) %collective-permute-start.2) | collective-permute-done | bytes 71712 | tf_op jit(solution)/shard_map/ppermute | solution.py:41
  13.8 2.3 %collective-permute-start.7 = (bf16[1,5,7168]{2,0,1:T(2,128)(2,1)S(1)}, bf16[1,5,7168]{2,0,1:T(2,128)(2,1)S(1)}, u32[]{:S(2)}, u32[]{:S(2)}) collective-permute-start(bf16[1,5,7168]{2,0,1:T(2,128)(2,1)S(1)} %get-tuple-element.12), channel_id=1, source_target_pairs={{0,8},{1,9},{2,10},{3,11},{4,12},{5,13},{6,14},{7,15},{8,0},{9,1},... | collective-permute-start | bytes 215048 | tf_op jit(solution)/shard_map/ppermute | solution.py:41
  16.2 0.2 collective-permute-start.8
  16.5 2.3 %collective-permute-start.9 = (bf16[1,5,7168]{2,0,1:T(2,128)(2,1)S(1)}, bf16[1,5,7168]{2,0,1:T(2,128)(2,1)S(1)}, u32[]{:S(2)}, u32[]{:S(2)}) collective-permute-start(bf16[1,5,7168]{2,0,1:T(2,128)(2,1)S(1)} %get-tuple-element.10), channel_id=1, source_target_pairs={{0,10},{1,11},{2,8},{3,9},{4,14},{5,15},{6,12},{7,13},{8,2},{9,3},... | collective-permute-start | bytes 215048 | tf_op jit(solution)/shard_map/ppermute | solution.py:41
  18.8 2.8 %collective-permute-done.5 = bf16[1,5,7168]{2,0,1:T(2,128)(2,1)S(1)} collective-permute-done((bf16[1,5,7168]{2,0,1:T(2,128)(2,1)S(1)}, bf16[1,5,7168]{2,0,1:T(2,128)(2,1)S(1)}, u32[]{:S(2)}, u32[]{:S(2)}) %collective-permute-start.5) | collective-permute-done | bytes 71712 | tf_op jit(solution)/shard_map/ppermute | solution.py:41
  21.7 5.0 %collective-permute-start.10 = (bf16[1,5,7168]{2,0,1:T(2,128)(2,1)S(1)}, bf16[1,5,7168]{2,0,1:T(2,128)(2,1)S(1)}, u32[]{:S(2)}, u32[]{:S(2)}) collective-permute-start(bf16[1,5,7168]{2,0,1:T(2,128)(2,1)S(1)} %get-tuple-element.9), channel_id=1, source_target_pairs={{0,11},{1,10},{2,9},{3,8},{4,15},{5,14},{6,13},{7,12},{8,3},{9,2},... | collective-permute-start | bytes 215048 | tf_op jit(solution)/shard_map/ppermute | solution.py:41
  26.7 1.4 collective-permute-start.11
  28.3 12.6 %collective-permute-done.8 = bf16[1,5,7168]{2,0,1:T(2,128)(2,1)S(1)} collective-permute-done((bf16[1,5,7168]{2,0,1:T(2,128)(2,1)S(1)}, bf16[1,5,7168]{2,0,1:T(2,128)(2,1)S(1)}, u32[]{:S(2)}, u32[]{:S(2)}) %collective-permute-start.8) | collective-permute-done | bytes 71712 | tf_op jit(solution)/shard_map/ppermute | solution.py:41
  41.0 3.0 %collective-permute-done.9 = bf16[1,5,7168]{2,0,1:T(2,128)(2,1)S(1)} collective-permute-done((bf16[1,5,7168]{2,0,1:T(2,128)(2,1)S(1)}, bf16[1,5,7168]{2,0,1:T(2,128)(2,1)S(1)}, u32[]{:S(2)}, u32[]{:S(2)}) %collective-permute-start.9) | collective-permute-done | bytes 71712 | tf_op jit(solution)/shard_map/ppermute | solution.py:41
  44.0 0.6 collective-permute-start.14
  44.6 5.5 %collective-permute-done.10 = bf16[1,5,7168]{2,0,1:T(2,128)(2,1)S(1)} collective-permute-done((bf16[1,5,7168]{2,0,1:T(2,128)(2,1)S(1)}, bf16[1,5,7168]{2,0,1:T(2,128)(2,1)S(1)}, u32[]{:S(2)}, u32[]{:S(2)}) %collective-permute-start.10) | collective-permute-done | bytes 71712 | tf_op jit(solution)/shard_map/ppermute | solution.py:41
  50.2 6.1 %collective-permute-done.11 = bf16[1,5,7168]{2,0,1:T(2,128)(2,1)S(1)} collective-permute-done((bf16[1,5,7168]{2,0,1:T(2,128)(2,1)S(1)}, bf16[1,5,7168]{2,0,1:T(2,128)(2,1)S(1)}, u32[]{:S(2)}, u32[]{:S(2)}) %collective-permute-start.11) | collective-permute-done | bytes 71712 | tf_op jit(solution)/shard_map/ppermute | solution.py:41
  56.3 3.4 %collective-permute-done.12 = bf16[1,5,7168]{2,0,1:T(2,128)(2,1)S(1)} collective-permute-done((bf16[1,5,7168]{2,0,1:T(2,128)(2,1)S(1)}, bf16[1,5,7168]{2,0,1:T(2,128)(2,1)S(1)}, u32[]{:S(2)}, u32[]{:S(2)}) %collective-permute-start.12) | collective-permute-done | bytes 71712 | tf_op jit(solution)/shard_map/ppermute | solution.py:41
  59.8 2.6 %collective-permute-done.13 = bf16[1,5,7168]{2,0,1:T(2,128)(2,1)S(1)} collective-permute-done((bf16[1,5,7168]{2,0,1:T(2,128)(2,1)S(1)}, bf16[1,5,7168]{2,0,1:T(2,128)(2,1)S(1)}, u32[]{:S(2)}, u32[]{:S(2)}) %collective-permute-start.13) | collective-permute-done | bytes 71712 | tf_op jit(solution)/shard_map/ppermute | solution.py:41
  62.5 3.0 %collective-permute-done.14 = bf16[1,5,7168]{2,0,1:T(2,128)(2,1)S(1)} collective-permute-done((bf16[1,5,7168]{2,0,1:T(2,128)(2,1)S(1)}, bf16[1,5,7168]{2,0,1:T(2,128)(2,1)S(1)}, u32[]{:S(2)}, u32[]{:S(2)}) %collective-permute-start.14) | collective-permute-done | bytes 71712 | tf_op jit(solution)/shard_map/ppermute | solution.py:41
  65.6 0.6 reshape.23
  66.1 12.9 %fusion.19 = f32[80,2048]{1,0:T(8,128)} fusion(bf16[80,7168]{1,0:T(8,128)(2,1)S(1)} %reshape.23, bf16[7168,2048]{1,0:T(8,128)(2,1)} %param.9), kind=kOutput, calls=%fused_computation.57 | convolution fusion | flops 2348810240 | bytes 31162368 | tf_op jit(solution)/shard_map/dot_general | solution.py:45
  79.0 21.0 %fusion.2 = f32[80,7168]{1,0:T(8,128)S(1)} fusion(bf16[2048,7168]{1,0:T(8,128)(2,1)} %param.11, f32[80,2048]{1,0:T(8,128)} %fusion.19, bf16[80,7168]{1,0:T(8,128)(2,1)S(1)} %reshape.23, bf16[7168,2048]{1,0:T(8,128)(2,1)} %param.10), kind=kOutput, calls=%fused_computation.5 | convolution fusion | flops 4698603520 | bytes 62816256 | tf_op jit(solution)/shard_map/dot_general | solution.py:48
  100.0 2.1 %reshape.24 = f32[16,5,7168]{2,1,0:T(8,128)} reshape(f32[80,7168]{1,0:T(8,128)S(1)} %fusion.2) | data formatting | bytes 4587520 | tf_op jit(solution)/shard_map/reshape | solution.py:49
  102.1 6.3 %all-to-all-start = ((f32[16,5,7168]{2,1,0:T(8,128)}), f32[16,5,7168]{2,1,0:T(8,128)}, u32[]{:S(2)}, u32[]{:S(2)}) async-start(f32[16,5,7168]{2,1,0:T(8,128)} %reshape.24), calls=%async_computation | async-start | bytes 7340032 | tf_op jit(solution)/shard_map/all_to_all | solution.py:50
  108.5 81.3 %all-to-all-done = f32[16,5,7168]{2,1,0:T(8,128)} async-done(((f32[16,5,7168]{2,1,0:T(8,128)}), f32[16,5,7168]{2,1,0:T(8,128)}, u32[]{:S(2)}, u32[]{:S(2)}) %all-to-all-start) | async-done | bytes 2293792 | tf_op jit(solution)/shard_map/all_to_all | solution.py:50
  189.9 6.2 %fusion = bf16[8,7168]{1,0:T(8,128)(2,1)} fusion(f32[16,5,7168]{2,1,0:T(8,128)} %all-to-all-done, f32[8,16]{1,0:T(8,128)S(1)} %select_reduce_fusion, s32[8,16]{1,0:T(8,128)S(1)} %copy-done.3, pred[8,16]{1,0:T(8,128)(4,1)S(1)} %copy-done.6), kind=kOutput, calls=%fused_computation.2 | convolution fusion | flops 55109504 | bytes 2409600 | tf_op jit(solution)/shard_map/tec,escd->td/dot_general | solution.py:52
  (45 shorter events, 1.2 us)
Async XLA Ops:
  0.0 1.0 copy-start
  0.8 3.3 %copy-start.5 = (pred[8,16]{1,0:T(8,128)(4,1)}, pred[8,16]{1,0:T(8,128)(4,1)S(1)}, u32[]{:S(2)}) copy-start(pred[8,16]{1,0:T(8,128)(4,1)S(1)} %broadcast_compare_fusion) | copy-start | bytes 388
  0.9 3.3 %copy-start.2 = (s32[8,16]{1,0:T(8,128)}, s32[8,16]{1,0:T(8,128)S(1)}, u32[]{:S(2)}) copy-start(s32[8,16]{1,0:T(8,128)S(1)} %broadcast_add_fusion) | copy-start | bytes 1540
  4.2 4.5 %collective-permute-start = (bf16[1,5,7168]{2,0,1:T(2,128)(2,1)S(1)}, bf16[1,5,7168]{2,0,1:T(2,128)(2,1)S(1)}, u32[]{:S(2)}, u32[]{:S(2)}) collective-permute-start(bf16[1,5,7168]{2,0,1:T(2,128)(2,1)S(1)} %get-tuple-element.19), channel_id=1, source_target_pairs={{0,1},{1,0},{2,3},{3,2},{4,5},{5,4},{6,7},{7,6},{8,9},{9,8},{10,11... | collective-permute-start | bytes 215048 | tf_op jit(solution)/shard_map/ppermute | solution.py:41
  4.9 5.3 %collective-permute-start.1 = (bf16[1,5,7168]{2,0,1:T(2,128)(2,1)S(1)}, bf16[1,5,7168]{2,0,1:T(2,128)(2,1)S(1)}, u32[]{:S(2)}, u32[]{:S(2)}) collective-permute-start(bf16[1,5,7168]{2,0,1:T(2,128)(2,1)S(1)} %get-tuple-element.18), channel_id=1, source_target_pairs={{0,2},{1,3},{2,0},{3,1},{4,6},{5,7},{6,4},{7,5},{8,10},{9,11},{10,... | collective-permute-start | bytes 215048 | tf_op jit(solution)/shard_map/ppermute | solution.py:41
  5.2 8.6 %collective-permute-start.2 = (bf16[1,5,7168]{2,0,1:T(2,128)(2,1)S(1)}, bf16[1,5,7168]{2,0,1:T(2,128)(2,1)S(1)}, u32[]{:S(2)}, u32[]{:S(2)}) collective-permute-start(bf16[1,5,7168]{2,0,1:T(2,128)(2,1)S(1)} %get-tuple-element.17), channel_id=1, source_target_pairs={{0,3},{1,2},{2,1},{3,0},{4,7},{5,6},{6,5},{7,4},{8,11},{9,10},{10,... | collective-permute-start | bytes 215048 | tf_op jit(solution)/shard_map/ppermute | solution.py:41
  6.7 9.5 %collective-permute-start.3 = (bf16[1,5,7168]{2,0,1:T(2,128)(2,1)S(1)}, bf16[1,5,7168]{2,0,1:T(2,128)(2,1)S(1)}, u32[]{:S(2)}, u32[]{:S(2)}) collective-permute-start(bf16[1,5,7168]{2,0,1:T(2,128)(2,1)S(1)} %get-tuple-element.16), channel_id=1, source_target_pairs={{0,4},{1,5},{2,6},{3,7},{4,0},{5,1},{6,2},{7,3},{8,12},{9,13},{10,... | collective-permute-start | bytes 215048 | tf_op jit(solution)/shard_map/ppermute | solution.py:41
  6.8 9.6 %collective-permute-start.4 = (bf16[1,5,7168]{2,0,1:T(2,128)(2,1)S(1)}, bf16[1,5,7168]{2,0,1:T(2,128)(2,1)S(1)}, u32[]{:S(2)}, u32[]{:S(2)}) collective-permute-start(bf16[1,5,7168]{2,0,1:T(2,128)(2,1)S(1)} %get-tuple-element.15), channel_id=1, source_target_pairs={{0,5},{1,4},{2,7},{3,6},{4,1},{5,0},{6,3},{7,2},{8,13},{9,12},{10,... | collective-permute-start | bytes 215048 | tf_op jit(solution)/shard_map/ppermute | solution.py:41
  8.7 13.0 %collective-permute-start.5 = (bf16[1,5,7168]{2,0,1:T(2,128)(2,1)S(1)}, bf16[1,5,7168]{2,0,1:T(2,128)(2,1)S(1)}, u32[]{:S(2)}, u32[]{:S(2)}) collective-permute-start(bf16[1,5,7168]{2,0,1:T(2,128)(2,1)S(1)} %get-tuple-element.14), channel_id=1, source_target_pairs={{0,6},{1,7},{2,4},{3,5},{4,2},{5,3},{6,0},{7,1},{8,14},{9,15},{10,... | collective-permute-start | bytes 215048 | tf_op jit(solution)/shard_map/ppermute | solution.py:41
  10.3 16.5 %collective-permute-start.6 = (bf16[1,5,7168]{2,0,1:T(2,128)(2,1)S(1)}, bf16[1,5,7168]{2,0,1:T(2,128)(2,1)S(1)}, u32[]{:S(2)}, u32[]{:S(2)}) collective-permute-start(bf16[1,5,7168]{2,0,1:T(2,128)(2,1)S(1)} %get-tuple-element.13), channel_id=1, source_target_pairs={{0,7},{1,6},{2,5},{3,4},{4,3},{5,2},{6,1},{7,0},{8,15},{9,14},{10,... | collective-permute-start | bytes 215048 | tf_op jit(solution)/shard_map/ppermute | solution.py:41
  13.8 14.4 %collective-permute-start.7 = (bf16[1,5,7168]{2,0,1:T(2,128)(2,1)S(1)}, bf16[1,5,7168]{2,0,1:T(2,128)(2,1)S(1)}, u32[]{:S(2)}, u32[]{:S(2)}) collective-permute-start(bf16[1,5,7168]{2,0,1:T(2,128)(2,1)S(1)} %get-tuple-element.12), channel_id=1, source_target_pairs={{0,8},{1,9},{2,10},{3,11},{4,12},{5,13},{6,14},{7,15},{8,0},{9,1},... | collective-permute-start | bytes 215048 | tf_op jit(solution)/shard_map/ppermute | solution.py:41
  16.2 24.8 %collective-permute-start.8 = (bf16[1,5,7168]{2,0,1:T(2,128)(2,1)S(1)}, bf16[1,5,7168]{2,0,1:T(2,128)(2,1)S(1)}, u32[]{:S(2)}, u32[]{:S(2)}) collective-permute-start(bf16[1,5,7168]{2,0,1:T(2,128)(2,1)S(1)} %get-tuple-element.11), channel_id=1, source_target_pairs={{0,9},{1,8},{2,11},{3,10},{4,13},{5,12},{6,15},{7,14},{8,1},{9,0},... | collective-permute-start | bytes 215048 | tf_op jit(solution)/shard_map/ppermute | solution.py:41
  16.5 27.6 %collective-permute-start.9 = (bf16[1,5,7168]{2,0,1:T(2,128)(2,1)S(1)}, bf16[1,5,7168]{2,0,1:T(2,128)(2,1)S(1)}, u32[]{:S(2)}, u32[]{:S(2)}) collective-permute-start(bf16[1,5,7168]{2,0,1:T(2,128)(2,1)S(1)} %get-tuple-element.10), channel_id=1, source_target_pairs={{0,10},{1,11},{2,8},{3,9},{4,14},{5,15},{6,12},{7,13},{8,2},{9,3},... | collective-permute-start | bytes 215048 | tf_op jit(solution)/shard_map/ppermute | solution.py:41
  21.7 28.5 %collective-permute-start.10 = (bf16[1,5,7168]{2,0,1:T(2,128)(2,1)S(1)}, bf16[1,5,7168]{2,0,1:T(2,128)(2,1)S(1)}, u32[]{:S(2)}, u32[]{:S(2)}) collective-permute-start(bf16[1,5,7168]{2,0,1:T(2,128)(2,1)S(1)} %get-tuple-element.9), channel_id=1, source_target_pairs={{0,11},{1,10},{2,9},{3,8},{4,15},{5,14},{6,13},{7,12},{8,3},{9,2},... | collective-permute-start | bytes 215048 | tf_op jit(solution)/shard_map/ppermute | solution.py:41
  26.7 29.6 %collective-permute-start.11 = (bf16[1,5,7168]{2,0,1:T(2,128)(2,1)S(1)}, bf16[1,5,7168]{2,0,1:T(2,128)(2,1)S(1)}, u32[]{:S(2)}, u32[]{:S(2)}) collective-permute-start(bf16[1,5,7168]{2,0,1:T(2,128)(2,1)S(1)} %get-tuple-element.8), channel_id=1, source_target_pairs={{0,12},{1,13},{2,14},{3,15},{4,8},{5,9},{6,10},{7,11},{8,4},{9,5},... | collective-permute-start | bytes 215048 | tf_op jit(solution)/shard_map/ppermute | solution.py:41
  28.2 31.6 %collective-permute-start.12 = (bf16[1,5,7168]{2,0,1:T(2,128)(2,1)S(1)}, bf16[1,5,7168]{2,0,1:T(2,128)(2,1)S(1)}, u32[]{:S(2)}, u32[]{:S(2)}) collective-permute-start(bf16[1,5,7168]{2,0,1:T(2,128)(2,1)S(1)} %get-tuple-element.7), channel_id=1, source_target_pairs={{0,13},{1,12},{2,15},{3,14},{4,9},{5,8},{6,11},{7,10},{8,5},{9,4},... | collective-permute-start | bytes 215048 | tf_op jit(solution)/shard_map/ppermute | solution.py:41
  40.9 21.5 %collective-permute-start.13 = (bf16[1,5,7168]{2,0,1:T(2,128)(2,1)S(1)}, bf16[1,5,7168]{2,0,1:T(2,128)(2,1)S(1)}, u32[]{:S(2)}, u32[]{:S(2)}) collective-permute-start(bf16[1,5,7168]{2,0,1:T(2,128)(2,1)S(1)} %get-tuple-element.6), channel_id=1, source_target_pairs={{0,14},{1,15},{2,12},{3,13},{4,10},{5,11},{6,8},{7,9},{8,6},{9,7},... | collective-permute-start | bytes 215048 | tf_op jit(solution)/shard_map/ppermute | solution.py:41
  44.0 21.5 %collective-permute-start.14 = (bf16[1,5,7168]{2,0,1:T(2,128)(2,1)S(1)}, bf16[1,5,7168]{2,0,1:T(2,128)(2,1)S(1)}, u32[]{:S(2)}, u32[]{:S(2)}) collective-permute-start(bf16[1,5,7168]{2,0,1:T(2,128)(2,1)S(1)} %get-tuple-element.5), channel_id=1, source_target_pairs={{0,15},{1,14},{2,13},{3,12},{4,11},{5,10},{6,9},{7,8},{8,7},{9,6},... | collective-permute-start | bytes 215048 | tf_op jit(solution)/shard_map/ppermute | solution.py:41
  102.1 6.3 %copy-start.4 = (s32[8,8]{1,0:T(8,128)S(1)}, s32[8,8]{1,0:T(8,128)}, u32[]{:S(2)}) copy-start(s32[8,8]{1,0:T(8,128)} %param.7) | copy-start | bytes 772
  102.1 6.3 %copy-start.7 = (f32[8,8]{1,0:T(8,128)S(1)}, f32[8,8]{1,0:T(8,128)}, u32[]{:S(2)}) copy-start(f32[8,8]{1,0:T(8,128)} %param.8) | copy-start | bytes 772
  102.1 87.8 %copy-start.3 = (s32[8,16]{1,0:T(8,128)S(1)}, s32[8,16]{1,0:T(8,128)}, u32[]{:S(2)}) copy-start(s32[8,16]{1,0:T(8,128)} %copy-done.2) | copy-start | bytes 1540
  102.1 87.8 %copy-start.6 = (pred[8,16]{1,0:T(8,128)(4,1)S(1)}, pred[8,16]{1,0:T(8,128)(4,1)}, u32[]{:S(2)}) copy-start(pred[8,16]{1,0:T(8,128)(4,1)} %copy-done.5) | copy-start | bytes 388
  102.1 87.8 %all-to-all-start = ((f32[16,5,7168]{2,1,0:T(8,128)}), f32[16,5,7168]{2,1,0:T(8,128)}, u32[]{:S(2)}, u32[]{:S(2)}) async-start(f32[16,5,7168]{2,1,0:T(8,128)} %reshape.24), calls=%async_computation | async-start | bytes 7340032 | tf_op jit(solution)/shard_map/all_to_all | solution.py:50
  108.4 87.6 %copy-start.1 = (bf16[8,7168]{1,0:T(8,128)(2,1)S(1)}, bf16[8,7168]{1,0:T(8,128)(2,1)}, u32[]{:S(2)}) copy-start(bf16[8,7168]{1,0:T(8,128)(2,1)} %param.6) | copy-start | bytes 344068
